TPU v7x, 512 devices: a whole 4x8x8 slice. The times are simulated.
512 devices in a mesh: row: 32 (over y, x), col: 16 (over z, core).
Axes of the slice: x: 4, y: 8, z: 8, core: 2. Of those that a mesh axis runs over, the one named last changes fastest.
Arguments:
- gram_panel: float32 [8192, 1024], P('row', 'col'), may hold values from -2973.8 to 2973.8, as said below
- left_factor: bfloat16 [8192, 16384], P('row', 'col'), may hold values from -0.42426407 to 0.42426407
- solved_prev: bfloat16 [16384, 8192], P('row', 'col'), may hold values from -0.59765625 to 0.59765625
- right_block: float32 [1024, 8192], P('row', 'col'), may hold values from -6 to 6
Outputs:
- panel_factor: float32 [8192, 1024], P('row', 'col')
- solved_panel: float32 [1024, 8192], P('row', 'col')
Inputs may be any that keep to these rules, and one draw needn't show every extreme that they name: The rows of gram_panel at the panel's indices minus the product of the corresponding rows of left_factor with their transpose form a symmetric positive definite matrix.
All inputs are finite; a program needn't handle non-finite values.
Results may differ from a plain program's by a relative error of at most 0.0006.
Values may be sent and summed in bfloat16 or wider, within the bound.
No kernel may reach another device: no remote copies, remote signals or barrier semaphores. Data moves between devices by JAX's collectives and lax.ppermute only.
A program may use at most 64 MiB of HBM per device.

v0:
```python
import jax
import jax.numpy as jnp
from jax import lax
from jax.sharding import PartitionSpec as P


def spread(value, axis, source):
    kept = jnp.where(lax.axis_index(axis) == source, value, 0).astype(value.dtype)
    return lax.psum(kept, axis)


def invert(diagonal):
    factor = jnp.linalg.cholesky(diagonal)
    identity = jnp.eye(diagonal.shape[0], dtype=jnp.float32)
    return jax.scipy.linalg.solve_triangular(factor, identity, lower=True)


def body(gram_panel, left_factor, solved_prev, right_block):
    row_count = lax.axis_size("row")
    col_count = lax.axis_size("col")
    row_place = lax.axis_index("row")
    col_place = lax.axis_index("col")
    block_rows = right_block.shape[0]
    col_width = gram_panel.shape[1]
    per_column = row_count // col_count
    strip_width = left_factor.shape[1] // per_column
    chosen = lax.all_gather(left_factor[:block_rows], "row", axis=0, tiled=True)
    portion = chosen
    summed = lax.psum_scatter(
        jnp.einsum("pk,mk->pm", portion, left_factor, preferred_element_type=jnp.float32),
        "col",
        scatter_dimension=0,
        tiled=True,
    )
    update = gram_panel - summed.T
    diag_part = lax.all_gather(update[:block_rows], "row", axis=0, tiled=True)
    diagonal = lax.all_gather(diag_part, "col", axis=1, tiled=True)
    inverse = invert(diagonal)
    inverse_cols = lax.dynamic_slice_in_dim(inverse, col_place * col_width, col_width, 0)
    inverse_part = inverse_cols
    panel_factor = lax.dot_general(
        lax.all_gather(update, "col", axis=1, tiled=True),
        inverse_part,
        (((1,), (1,)), ((), ())),
        precision=lax.Precision.HIGHEST,
    )
    strip_piece = lax.dynamic_slice_in_dim(
        chosen, row_place % per_column * strip_width, strip_width, 1
    )
    strip_piece = spread(strip_piece, "col", row_place // per_column)
    portion = strip_piece
    reduced = right_block - lax.psum_scatter(
        jnp.dot(portion, solved_prev, preferred_element_type=jnp.float32),
        "row",
        scatter_dimension=0,
        tiled=True,
    )
    inverse_rows = lax.dynamic_slice_in_dim(inverse, row_place * block_rows, block_rows, 0)
    inverse_part = inverse_rows
    solved_panel = jnp.dot(
        inverse_part,
        lax.all_gather(reduced, "row", axis=0, tiled=True),
        precision=lax.Precision.HIGHEST,
    )
    return (panel_factor, solved_panel)


def solution(mesh):
    in_specs = (P("row", "col"), P("row", "col"), P("row", "col"), P("row", "col"))
    out_specs = (P("row", "col"), P("row", "col"))
    return jax.shard_map(body, mesh=mesh, in_specs=in_specs, out_specs=out_specs, check_vma=False)
```

profile of v0, /device:TPU:1, one launch (start us, length us, event | category | flops | bytes accessed | tf_op | source)
XLA Modules:
  0.0 915.5 jit_solution(4656776217967420164)
XLA Ops:
  8.8 87.9 %all-gather.5.cloned.1.call-done = bf16[1024,1024]{1,0:T(8,128)(2,1)} async-done(((bf16[32,1024]{1,0:T(8,128)(2,1)}), bf16[1024,1024]{1,0:T(8,128)(2,1)}) %all-gather.5.cloned.1.call-update) | async-done | bytes 2097168 | tf_op jit(solution)/shard_map/all_gather | solution.py:27
  102.7 115.2 %all-reduce.3.cloned.1.call-done = bf16[1024,512]{1,0:T(8,128)(2,1)} async-done(((bf16[1024,512]{1,0:T(8,128)(2,1)}), bf16[1024,512]{1,0:T(8,128)(2,1)}) %all-reduce.3.cloned.1.call-update) | async-done | bytes 1048592 | tf_op jit(solution)/shard_map/psum | solution.py:9
  221.3 57.3 %reduce-scatter.3.cloned.1.call-done = f32[64,256]{1,0:T(8,128)} async-done(((f32[1024,256]{1,0:T(8,128)}), f32[64,256]{1,0:T(8,128)}) %reduce-scatter.3.cloned.1.call-update) | async-done | bytes 65552 | tf_op jit(solution)/shard_map/reduce_scatter | solution.py:29
  279.6 38.7 %all_gather.17 = f32[1024,64]{1,0:T(8,128)S(1)} all-gather(f32[32,64]{1,0:T(8,128)S(1)} %copy.7), channel_id=1, replica_groups=mesh['row'=32,'col'=16] {'row'}, dimensions={0}, use_global_device_ids=true | all-gather | bytes 270336 | tf_op jit(solution)/shard_map/all_gather | solution.py:36
  319.3 180.5 %reduce-scatter.5.cloned.1.call-done = f32[32,512]{1,0:T(8,128)} async-done(((f32[1024,512]{1,0:T(8,128)}), f32[32,512]{1,0:T(8,128)}) %reduce-scatter.5.cloned.1.call-update) | async-done | bytes 65552 | tf_op jit(solution)/shard_map/reduce_scatter | solution.py:52
  504.2 47.7 %all-gather.9.cloned.1.call-done = f32[1024,1024]{0,1:T(8,128)} async-done(((f32[1024,64]{0,1:T(8,128)}), f32[1024,1024]{0,1:T(8,128)}) %all-gather.9.cloned.1.call-update) | async-done | bytes 4194320 | tf_op jit(solution)/shard_map/all_gather | solution.py:37
  551.8 5.8 copy.9
  564.1 11.7 %cholesky.223 = f32[128,128]{1,0:T(8,128)S(1)} custom-call(f32[128,128]{1,0:T(8,128)S(1)} %cholesky.580), custom_call_target="Cholesky" | custom-call | tf_op jit(solution)/shard_map/jit(cholesky)/cholesky | solution.py:13
  575.9 9.8 %custom-call.63 = f32[1,128,128]{1,2,0:T(8,128)S(1)} custom-call(f32[1,128,128]{2,1,0:T(8,128)S(1)} %get-tuple-element.66), custom_call_target="InvertDiagBlocksLowerTriangular" | custom-call | tf_op jit(solution)/shard_map/jit(cholesky)/cholesky | solution.py:13
  592.1 11.9 %cholesky.244 = f32[128,128]{1,0:T(8,128)S(1)} custom-call(f32[128,128]{1,0:T(8,128)S(1)} %cholesky.584), custom_call_target="Cholesky" | custom-call | tf_op jit(solution)/shard_map/jit(cholesky)/cholesky | solution.py:13
  604.6 9.8 %custom-call.64 = f32[1,128,128]{1,2,0:T(8,128)S(1)} custom-call(f32[1,128,128]{2,1,0:T(8,128)S(1)} %get-tuple-element.63), custom_call_target="InvertDiagBlocksLowerTriangular" | custom-call | tf_op jit(solution)/shard_map/jit(cholesky)/cholesky | solution.py:13
  617.8 11.7 %cholesky.468 = f32[128,128]{1,0:T(8,128)S(1)} custom-call(f32[128,128]{1,0:T(8,128)S(1)} %cholesky.589), custom_call_target="Cholesky" | custom-call | tf_op jit(solution)/shard_map/jit(cholesky)/cholesky | solution.py:13
  630.8 9.8 %custom-call.65 = f32[1,128,128]{1,2,0:T(8,128)S(1)} custom-call(f32[1,128,128]{2,1,0:T(8,128)S(1)} %get-tuple-element.60), custom_call_target="InvertDiagBlocksLowerTriangular" | custom-call | tf_op jit(solution)/shard_map/jit(cholesky)/cholesky | solution.py:13
  644.2 11.9 %cholesky.487 = f32[128,128]{1,0:T(8,128)S(1)} custom-call(f32[128,128]{1,0:T(8,128)S(1)} %cholesky.594), custom_call_target="Cholesky" | custom-call | tf_op jit(solution)/shard_map/jit(cholesky)/cholesky | solution.py:13
  657.3 9.8 %custom-call.66 = f32[1,128,128]{1,2,0:T(8,128)S(1)} custom-call(f32[1,128,128]{2,1,0:T(8,128)S(1)} %get-tuple-element.57), custom_call_target="InvertDiagBlocksLowerTriangular" | custom-call | tf_op jit(solution)/shard_map/jit(cholesky)/cholesky | solution.py:13
  670.6 11.7 %cholesky.506 = f32[128,128]{1,0:T(8,128)S(1)} custom-call(f32[128,128]{1,0:T(8,128)S(1)} %cholesky.599), custom_call_target="Cholesky" | custom-call | tf_op jit(solution)/shard_map/jit(cholesky)/cholesky | solution.py:13
  683.6 10.2 %custom-call.67 = f32[1,128,128]{1,2,0:T(8,128)S(1)} custom-call(f32[1,128,128]{2,1,0:T(8,128)S(1)} %get-tuple-element.54), custom_call_target="InvertDiagBlocksLowerTriangular" | custom-call | tf_op jit(solution)/shard_map/jit(cholesky)/cholesky | solution.py:13
  697.1 11.7 %cholesky.526 = f32[128,128]{1,0:T(8,128)S(1)} custom-call(f32[128,128]{1,0:T(8,128)S(1)} %cholesky.604), custom_call_target="Cholesky" | custom-call | tf_op jit(solution)/shard_map/jit(cholesky)/cholesky | solution.py:13
  710.2 9.8 %custom-call.68 = f32[1,128,128]{1,2,0:T(8,128)S(1)} custom-call(f32[1,128,128]{2,1,0:T(8,128)S(1)} %get-tuple-element.51), custom_call_target="InvertDiagBlocksLowerTriangular" | custom-call | tf_op jit(solution)/shard_map/jit(cholesky)/cholesky | solution.py:13
  723.0 11.9 %cholesky.546 = f32[128,128]{1,0:T(8,128)S(1)} custom-call(f32[128,128]{1,0:T(8,128)S(1)} %cholesky.609), custom_call_target="Cholesky" | custom-call | tf_op jit(solution)/shard_map/jit(cholesky)/cholesky | solution.py:13
  736.2 9.8 %custom-call.69 = f32[1,128,128]{1,2,0:T(8,128)S(1)} custom-call(f32[1,128,128]{2,1,0:T(8,128)S(1)} %get-tuple-element.48), custom_call_target="InvertDiagBlocksLowerTriangular" | custom-call | tf_op jit(solution)/shard_map/jit(cholesky)/cholesky | solution.py:13
  748.7 11.7 %cholesky.564 = f32[128,128]{1,0:T(8,128)S(1)} custom-call(f32[128,128]{1,0:T(8,128)S(1)} %convolution_subtract_fusion.11), custom_call_target="Cholesky" | custom-call | tf_op jit(solution)/shard_map/jit(cholesky)/cholesky | solution.py:13
  772.3 22.5 %while.1 = (s32[]{:T(128)}, f32[1024,1024]{1,0:T(8,128)}, s32[8,2]{0,1:T(2,128)S(1)}, f32[8,128,128]{2,1,0:T(8,128)S(1)}, s32[]{:T(128)}) while((s32[]{:T(128)}, f32[1024,1024]{1,0:T(8,128)}, s32[8,2]{0,1:T(2,128)S(1)}, f32[8,128,128]{2,1,0:T(8,128)S(1)}, s32[]{:T(128)}) %tuple.61), condition=%wide.while_cond, body=%wide.while_body.sunk | while | flops 2 | bytes 131181 | solution.py:15
  794.7 78.8 %custom-call.70 = f32[8,128,128]{1,2,0:T(8,128)S(1)} custom-call(f32[8,128,128]{2,1,0:T(8,128)S(1)} %get-tuple-element.9), custom_call_target="InvertDiagBlocksLowerTriangular" | custom-call | tf_op jit(solution)/shard_map/jit(_solve_triangular)/triangular_solve | solution.py:15
  (122 shorter events, 120.3 us)
Async XLA Ops:
  7.2 210.8 %copy-start = (bf16[512,512]{1,0:T(8,128)(2,1)S(1)}, bf16[512,512]{1,0:T(8,128)(2,1)}, u32[]{:S(2)}) copy-start(bf16[512,512]{1,0:T(8,128)(2,1)} %param.6) | copy-start | bytes 1572868
  7.2 89.6 %all-gather.5.cloned.1.call-start = ((), (), s32[]{:S(2)}) async-start(), calls=%async_computation.2 | async-start | bytes 2162688 | tf_op jit(solution)/shard_map/all_gather | solution.py:27
  8.8 209.2 %all-reduce.3.cloned.1.call-start = ((), (), s32[]{:S(2)}) async-start(), calls=%async_computation.6 | async-start | bytes 2097152 | tf_op jit(solution)/shard_map/psum | solution.py:9
  99.2 179.5 %reduce-scatter.3.cloned.1.call-start = ((), (), s32[]{:S(2)}) async-start(), calls=%async_computation.3 | async-start | bytes 1114112 | tf_op jit(solution)/shard_map/reduce_scatter | solution.py:29
  102.6 176.0 %copy-start.4 = (f32[256,64]{0,1:T(8,128)S(1)}, f32[256,64]{0,1:T(8,128)}, u32[]{:S(2)}) copy-start(f32[256,64]{0,1:T(8,128)} %param.4) | copy-start | bytes 196612
  102.7 397.2 %copy-start.5 = (f32[32,512]{1,0:T(8,128)S(1)}, f32[32,512]{1,0:T(8,128)}, u32[]{:S(2)}) copy-start(f32[32,512]{1,0:T(8,128)} %param.7) | copy-start | bytes 196612
  102.7 397.1 %reduce-scatter.5.cloned.1.call-start = ((), (), s32[]{:S(2)}) async-start(), calls=%async_computation.7 | async-start | bytes 2162688 | tf_op jit(solution)/shard_map/reduce_scatter | solution.py:52
  221.3 330.6 %all-gather.9.cloned.1.call-start = ((), (), s32[]{:S(2)}) async-start(), calls=%async_computation.5 | async-start | bytes 4456448 | tf_op jit(solution)/shard_map/all_gather | solution.py:37
  279.5 224.6 %copy-start.3 = (f32[256,64]{0,1:T(8,128)}, f32[256,64]{0,1:T(8,128)S(1)}, u32[]{:S(2)}) copy-start(f32[256,64]{0,1:T(8,128)S(1)} %bitcast_subtract_fusion) | copy-start | bytes 196612
  319.2 582.9 %all-gather.11.cloned.1.call-start = ((), (), s32[]{:S(2)}) async-start(), calls=%async_computation.8 | async-start | bytes 2162688 | tf_op jit(solution)/shard_map/all_gather | solution.py:62
  501.3 404.4 %all-gather.7.cloned.1.call-start = ((), (), s32[]{:S(2)}) async-start(), calls=%async_computation.4 | async-start | bytes 1114112 | tf_op jit(solution)/shard_map/all_gather | solution.py:42
  562.1 2.0 copy-start.2
  873.6 4.7 copy-start.1
Sparse Core Ops, SparseCore 0:
  11.8 84.9 all-gather.4
  99.3 118.6 all-reduce.2
  221.0 57.5 reduce-scatter.2
  282.9 216.8 reduce-scatter.4
  502.0 49.8 all-gather.8
  555.9 77.5 all-gather.10
  636.4 43.9 all-gather.6
where the time goes:
time: 920 us; the launch traced here: 915 us
  waiting for transfers between devices  489 us (53%)
  other arithmetic  268 us (29%)
  matrix products  64.5 us (7%)
  blocking collectives  38.7 us (4%)
  local copies, waits for them, and re-layouts  35.2 us (4%)
  between operations  19.8 us (2%)
    reduce_scatter x1, waiting for transfers between devices, body(): lax.psum_scatter(jnp.dot(portion, solved_prev, preferred_element_type=jnp...  181 us
    another operation x30, other arithmetic, invert(): factor = jnp.linalg.cholesky(diagonal)  172 us
    psum x1, waiting for transfers between devices, spread(): return lax.psum(kept, axis)  115 us
    all_gather x1, waiting for transfers between devices, body(): chosen = lax.all_gather(left_factor[:block_rows], 'row', axis=0, tiled=True)  87.9 us
    another operation x3, other arithmetic, invert(): return jax.scipy.linalg.solve_triangular(factor, identity, lower=True)  83.6 us
    reduce_scatter x1, waiting for transfers between devices, body(): lax.psum_scatter(jnp.einsum('pk,mk->pm', portion, left_factor, preferred_...  57.3 us
    all_gather x1, waiting for transfers between devices, body(): diagonal = lax.all_gather(diag_part, 'col', axis=1, tiled=True)  47.7 us
    all_gather x1, blocking collectives, body(): diag_part = lax.all_gather(update[:block_rows], 'row', axis=0, tiled=True)  38.7 us
  transfers between devices with their start and end apart: 7, of which 5 were waited for; matrix products, arithmetic and copies ran while one was open for 39% of the time, Pallas kernels for 0%

commit v1 on v0

--- a/solution.py
+++ b/solution.py
@@ -34,7 +34,12 @@
     )
     update = gram_panel - summed.T
     diag_part = lax.all_gather(update[:block_rows], "row", axis=0, tiled=True)
-    diagonal = lax.all_gather(diag_part, "col", axis=1, tiled=True)
+    ring = [diag_part]
+    for hop in range(15):
+        ring.append(lax.ppermute(ring[-1], "col", [(dev, (dev + 1) % 16) for dev in range(16)]))
+    diagonal = jnp.roll(
+        jnp.concatenate(ring[::-1], axis=1), (lax.axis_index("col") + 1) * ring[0].shape[1], axis=1
+    )
     inverse = invert(diagonal)
     inverse_cols = lax.dynamic_slice_in_dim(inverse, col_place * col_width, col_width, 0)
     inverse_part = inverse_cols

time: 920 us -> 898 us (0.976)
  waiting for transfers between devices: 489 us -> 421 us
  local copies, waits for them, and re-layouts: 35.2 us -> 57.2 us
  starting transfers between devices: 0.29 us -> 16.9 us
    reduce_scatter x1, waiting for transfers between devices: 181 us -> 71.9 us  [body(): lax.psum_scatter(jnp.dot(portion, solved_prev, preferred_element_type=jnp...]
    ppermute x0 -> x15, waiting for transfers between devices: none -> 88.8 us  [body(): lax.ppermute(ring[-1], 'col', [(dev, (dev + 1) % 16) for dev in range(16)])]
    all_gather x1 -> x0, waiting for transfers between devices: 47.7 us -> none  [body(): diagonal = lax.all_gather(diag_part, 'col', axis=1, tiled=True)]
    ppermute x0 -> x15, starting transfers between devices: none -> 16.7 us  [body(): lax.ppermute(ring[-1], 'col', [(dev, (dev + 1) % 16) for dev in range(16)])]
    unnamed x12 -> x71, local copies, waits for them, and re-layouts: 1.99 us -> 16.4 us
  transfers between devices with their start and end apart: 7 -> 21, of which waited for: 5 -> 18; matrix products, arithmetic and copies ran while one was open for 39% -> 42% of each run, Pallas kernels for 0% -> 0%
where the time goes in v1:
time: 898 us; the launch traced here: 889 us
  waiting for transfers between devices  421 us (47%)
  other arithmetic  269 us (30%)
  matrix products  64.6 us (7%)
  local copies, waits for them, and re-layouts  57.2 us (6%)
  blocking collectives  39.3 us (4%)
  between operations  20.2 us (2%)
  starting transfers between devices  16.9 us (2%)
    another operation x30, other arithmetic, invert(): factor = jnp.linalg.cholesky(diagonal)  173 us
    psum x1, waiting for transfers between devices, spread(): return lax.psum(kept, axis)  115 us
    ppermute x15, waiting for transfers between devices, body(): lax.ppermute(ring[-1], 'col', [(dev, (dev + 1) % 16) for dev in range(16)])  88.8 us
    all_gather x1, waiting for transfers between devices, body(): chosen = lax.all_gather(left_factor[:block_rows], 'row', axis=0, tiled=True)  88 us
    another operation x3, other arithmetic, invert(): return jax.scipy.linalg.solve_triangular(factor, identity, lower=True)  84.4 us
    reduce_scatter x1, waiting for transfers between devices, body(): lax.psum_scatter(jnp.dot(portion, solved_prev, preferred_element_type=jnp...  71.9 us
    reduce_scatter x1, waiting for transfers between devices, body(): lax.psum_scatter(jnp.einsum('pk,mk->pm', portion, left_factor, preferred_...  57.3 us
    all_gather x1, blocking collectives, body(): diag_part = lax.all_gather(update[:block_rows], 'row', axis=0, tiled=True)  39.3 us
  transfers between devices with their start and end apart: 21, of which 18 were waited for; matrix products, arithmetic and copies ran while one was open for 42% of the time, Pallas kernels for 0%

profile of v1, /device:TPU:1, one launch (start us, length us, event | category | flops | bytes accessed | tf_op | source)
XLA Modules:
  0.0 888.6 jit_solution(15251062687598436001)
XLA Ops:
  8.9 88.0 %all-gather.4.cloned.1.call-done = bf16[1024,1024]{1,0:T(8,128)(2,1)} async-done(((bf16[32,1024]{1,0:T(8,128)(2,1)}), bf16[1024,1024]{1,0:T(8,128)(2,1)}) %all-gather.4.cloned.1.call-update) | async-done | bytes 2097168 | tf_op jit(solution)/shard_map/all_gather | solution.py:27
  102.7 115.3 %all-reduce.3.cloned.1.call-done = bf16[1024,512]{1,0:T(8,128)(2,1)} async-done(((bf16[1024,512]{1,0:T(8,128)(2,1)}), bf16[1024,512]{1,0:T(8,128)(2,1)}) %all-reduce.3.cloned.1.call-update) | async-done | bytes 1048592 | tf_op jit(solution)/shard_map/psum | solution.py:9
  221.4 57.3 %reduce-scatter.3.cloned.1.call-done = f32[64,256]{1,0:T(8,128)} async-done(((f32[1024,256]{1,0:T(8,128)}), f32[64,256]{1,0:T(8,128)}) %reduce-scatter.3.cloned.1.call-update) | async-done | bytes 65552 | tf_op jit(solution)/shard_map/reduce_scatter | solution.py:29
  279.6 39.3 %all_gather.14 = f32[1024,64]{1,0:T(8,128)S(1)} all-gather(f32[32,64]{1,0:T(8,128)S(1)} %copy.7), channel_id=1, replica_groups=mesh['row'=32,'col'=16] {'row'}, dimensions={0}, use_global_device_ids=true | all-gather | bytes 270336 | tf_op jit(solution)/shard_map/all_gather | solution.py:36
  319.1 12.2 %collective-permute-start = (f32[1024,64]{0,1:T(8,128)S(1)}, f32[1024,64]{0,1:T(8,128)S(1)}, u32[]{:S(2)}, u32[]{:S(2)}) collective-permute-start(f32[1024,64]{0,1:T(8,128)S(1)} %copy.8), channel_id=1, source_target_pairs={{0,1},{1,2},{2,3},{3,4},{4,5},{5,6},{6,7},{7,8},{8,9},{9,10},{10,1... | collective-permute-start | bytes 786440 | tf_op jit(solution)/shard_map/ppermute | solution.py:39
  383.4 7.0 collective-permute-done.8
  428.1 71.9 %reduce-scatter.5.cloned.1.call-done = f32[32,512]{1,0:T(8,128)} async-done(((f32[1024,512]{1,0:T(8,128)}), f32[32,512]{1,0:T(8,128)}) %reduce-scatter.5.cloned.1.call-update) | async-done | bytes 65552 | tf_op jit(solution)/shard_map/reduce_scatter | solution.py:57
  530.2 11.7 %cholesky.223 = f32[128,128]{1,0:T(8,128)S(1)} custom-call(f32[128,128]{1,0:T(8,128)S(1)} %cholesky.580), custom_call_target="Cholesky" | custom-call | tf_op jit(solution)/shard_map/jit(cholesky)/cholesky | solution.py:13
  544.4 9.8 %custom-call.63 = f32[1,128,128]{1,2,0:T(8,128)S(1)} custom-call(f32[1,128,128]{2,1,0:T(8,128)S(1)} %get-tuple-element.66), custom_call_target="InvertDiagBlocksLowerTriangular" | custom-call | tf_op jit(solution)/shard_map/jit(cholesky)/cholesky | solution.py:13
  558.2 11.9 %cholesky.244 = f32[128,128]{1,0:T(8,128)S(1)} custom-call(f32[128,128]{1,0:T(8,128)S(1)} %cholesky.584), custom_call_target="Cholesky" | custom-call | tf_op jit(solution)/shard_map/jit(cholesky)/cholesky | solution.py:13
  570.7 9.8 %custom-call.64 = f32[1,128,128]{1,2,0:T(8,128)S(1)} custom-call(f32[1,128,128]{2,1,0:T(8,128)S(1)} %get-tuple-element.63), custom_call_target="InvertDiagBlocksLowerTriangular" | custom-call | tf_op jit(solution)/shard_map/jit(cholesky)/cholesky | solution.py:13
  583.9 11.7 %cholesky.468 = f32[128,128]{1,0:T(8,128)S(1)} custom-call(f32[128,128]{1,0:T(8,128)S(1)} %cholesky.589), custom_call_target="Cholesky" | custom-call | tf_op jit(solution)/shard_map/jit(cholesky)/cholesky | solution.py:13
  596.9 9.8 %custom-call.65 = f32[1,128,128]{1,2,0:T(8,128)S(1)} custom-call(f32[1,128,128]{2,1,0:T(8,128)S(1)} %get-tuple-element.60), custom_call_target="InvertDiagBlocksLowerTriangular" | custom-call | tf_op jit(solution)/shard_map/jit(cholesky)/cholesky | solution.py:13
  610.3 11.9 %cholesky.487 = f32[128,128]{1,0:T(8,128)S(1)} custom-call(f32[128,128]{1,0:T(8,128)S(1)} %cholesky.594), custom_call_target="Cholesky" | custom-call | tf_op jit(solution)/shard_map/jit(cholesky)/cholesky | solution.py:13
  623.5 9.8 %custom-call.66 = f32[1,128,128]{1,2,0:T(8,128)S(1)} custom-call(f32[1,128,128]{2,1,0:T(8,128)S(1)} %get-tuple-element.57), custom_call_target="InvertDiagBlocksLowerTriangular" | custom-call | tf_op jit(solution)/shard_map/jit(cholesky)/cholesky | solution.py:13
  636.8 11.7 %cholesky.506 = f32[128,128]{1,0:T(8,128)S(1)} custom-call(f32[128,128]{1,0:T(8,128)S(1)} %cholesky.599), custom_call_target="Cholesky" | custom-call | tf_op jit(solution)/shard_map/jit(cholesky)/cholesky | solution.py:13
  649.9 10.2 %custom-call.67 = f32[1,128,128]{1,2,0:T(8,128)S(1)} custom-call(f32[1,128,128]{2,1,0:T(8,128)S(1)} %get-tuple-element.54), custom_call_target="InvertDiagBlocksLowerTriangular" | custom-call | tf_op jit(solution)/shard_map/jit(cholesky)/cholesky | solution.py:13
  663.4 11.7 %cholesky.526 = f32[128,128]{1,0:T(8,128)S(1)} custom-call(f32[128,128]{1,0:T(8,128)S(1)} %cholesky.604), custom_call_target="Cholesky" | custom-call | tf_op jit(solution)/shard_map/jit(cholesky)/cholesky | solution.py:13
  676.4 9.8 %custom-call.68 = f32[1,128,128]{1,2,0:T(8,128)S(1)} custom-call(f32[1,128,128]{2,1,0:T(8,128)S(1)} %get-tuple-element.51), custom_call_target="InvertDiagBlocksLowerTriangular" | custom-call | tf_op jit(solution)/shard_map/jit(cholesky)/cholesky | solution.py:13
  689.3 11.9 %cholesky.546 = f32[128,128]{1,0:T(8,128)S(1)} custom-call(f32[128,128]{1,0:T(8,128)S(1)} %cholesky.609), custom_call_target="Cholesky" | custom-call | tf_op jit(solution)/shard_map/jit(cholesky)/cholesky | solution.py:13
  702.5 9.8 %custom-call.69 = f32[1,128,128]{1,2,0:T(8,128)S(1)} custom-call(f32[1,128,128]{2,1,0:T(8,128)S(1)} %get-tuple-element.48), custom_call_target="InvertDiagBlocksLowerTriangular" | custom-call | tf_op jit(solution)/shard_map/jit(cholesky)/cholesky | solution.py:13
  715.0 11.7 %cholesky.564 = f32[128,128]{1,0:T(8,128)S(1)} custom-call(f32[128,128]{1,0:T(8,128)S(1)} %slice_subtract_fusion.6), custom_call_target="Cholesky" | custom-call | tf_op jit(solution)/shard_map/jit(cholesky)/cholesky | solution.py:13
  738.6 28.3 %while.1 = (s32[]{:T(128)}, f32[1024,1024]{1,0:T(8,128)}, s32[8,2]{0,1:T(2,128)S(1)}, f32[8,128,128]{2,1,0:T(8,128)}, s32[]{:T(128)}) while((s32[]{:T(128)}, f32[1024,1024]{1,0:T(8,128)}, s32[8,2]{0,1:T(2,128)S(1)}, f32[8,128,128]{2,1,0:T(8,128)}, s32[]{:T(128)}) %tuple.61), condition=%wide.while_cond, body=%wide.while_body.sunk | while | flops 2 | bytes 132705 | solution.py:15
  767.0 79.6 %custom-call.70 = f32[8,128,128]{1,2,0:T(8,128)S(1)} custom-call(f32[8,128,128]{2,1,0:T(8,128)} %get-tuple-element.9), custom_call_target="InvertDiagBlocksLowerTriangular" | custom-call | tf_op jit(solution)/shard_map/jit(_solve_triangular)/triangular_solve | solution.py:15
  (210 shorter events, 234.6 us)
Async XLA Ops:
  7.2 210.9 %copy-start = (bf16[512,512]{1,0:T(8,128)(2,1)S(1)}, bf16[512,512]{1,0:T(8,128)(2,1)}, u32[]{:S(2)}) copy-start(bf16[512,512]{1,0:T(8,128)(2,1)} %param.6) | copy-start | bytes 1572868
  7.2 89.6 %all-gather.4.cloned.1.call-start = ((), (), s32[]{:S(2)}) async-start(), calls=%async_computation.2 | async-start | bytes 2162688 | tf_op jit(solution)/shard_map/all_gather | solution.py:27
  8.8 209.2 %all-reduce.3.cloned.1.call-start = ((), (), s32[]{:S(2)}) async-start(), calls=%async_computation.5 | async-start | bytes 2097152 | tf_op jit(solution)/shard_map/psum | solution.py:9
  99.2 179.5 %reduce-scatter.3.cloned.1.call-start = ((), (), s32[]{:S(2)}) async-start(), calls=%async_computation.3 | async-start | bytes 1114112 | tf_op jit(solution)/shard_map/reduce_scatter | solution.py:29
  102.7 176.1 %copy-start.18 = (f32[256,64]{0,1:T(8,128)S(1)}, f32[256,64]{0,1:T(8,128)}, u32[]{:S(2)}) copy-start(f32[256,64]{0,1:T(8,128)} %param.4) | copy-start | bytes 196612
  102.7 397.3 %reduce-scatter.5.cloned.1.call-start = ((), (), s32[]{:S(2)}) async-start(), calls=%async_computation.6 | async-start | bytes 2162688 | tf_op jit(solution)/shard_map/reduce_scatter | solution.py:57
  221.3 278.7 %copy-start.19 = (f32[32,512]{1,0:T(8,128)S(1)}, f32[32,512]{1,0:T(8,128)}, u32[]{:S(2)}) copy-start(f32[32,512]{1,0:T(8,128)} %param.7) | copy-start | bytes 196612
  221.3 653.9 %all-gather.6.cloned.1.call-start = ((), (), s32[]{:S(2)}) async-start(), calls=%async_computation.4 | async-start | bytes 1114112 | tf_op jit(solution)/shard_map/all_gather | solution.py:47
  319.1 15.5 %collective-permute-start = (f32[1024,64]{0,1:T(8,128)S(1)}, f32[1024,64]{0,1:T(8,128)S(1)}, u32[]{:S(2)}, u32[]{:S(2)}) collective-permute-start(f32[1024,64]{0,1:T(8,128)S(1)} %copy.8), channel_id=1, source_target_pairs={{0,1},{1,2},{2,3},{3,4},{4,5},{5,6},{6,7},{7,8},{8,9},{9,10},{10,1... | collective-permute-start | bytes 786440 | tf_op jit(solution)/shard_map/ppermute | solution.py:39
  334.6 6.7 collective-permute-start.1
  341.4 7.0 collective-permute-start.2
  348.4 7.0 collective-permute-start.3
  355.4 7.0 collective-permute-start.4
  362.4 7.0 collective-permute-start.5
  369.4 7.0 collective-permute-start.6
  376.4 7.0 collective-permute-start.7
  376.4 501.4 %all-gather.8.cloned.1.call-start = ((), (), s32[]{:S(2)}) async-start(), calls=%async_computation.7 | async-start | bytes 2162688 | tf_op jit(solution)/shard_map/all_gather | solution.py:67
  383.4 7.0 collective-permute-start.8
  390.4 7.0 collective-permute-start.9
  397.4 7.0 collective-permute-start.10
  404.4 7.0 collective-permute-start.11
  411.4 7.0 collective-permute-start.12
  418.5 7.2 collective-permute-start.13
  425.7 75.9 %collective-permute-start.14 = (f32[1024,64]{0,1:T(8,128)}, f32[1024,64]{0,1:T(8,128)}, u32[]{:S(2)}, u32[]{:S(2)}) collective-permute-start(f32[1024,64]{0,1:T(8,128)} %collective-permute-done.13), channel_id=1, source_target_pairs={{0,1},{1,2},{2,3},{3,4},{4,5},{5,6},{6,7},{7,8},{8,9},{9,10},{10,1... | collective-permute-start | bytes 786440 | tf_op jit(solution)/shard_map/ppermute | solution.py:39
  (17 other events, 259.4 us)
Sparse Core Ops, SparseCore 0:
  11.8 85.0 all-gather.3
  99.3 118.6 all-reduce.2
  221.1 57.5 reduce-scatter.2
  283.0 216.9 reduce-scatter.4
  502.8 46.2 all-gather.5
  552.5 77.3 all-gather.7
